TPU v7x, 128 devices: a whole 4x4x4 slice. The times are simulated.
128 devices in a mesh: prow: 8 (over y, core), pcol: 16 (over x, z).
Axes of the slice: x: 4, y: 4, z: 4, core: 2. Of those that a mesh axis runs over, the one named last changes fastest.
Arguments:
- cross_cov: float32 [2, 512, 16384], P(None, 'prow', 'pcol'), may hold values from -6 to 6
- prev_rows: bfloat16 [2, 512, 32768], P(None, 'pcol', 'prow'), may hold values from -0.046875 to 0.046875
- prev_solved: bfloat16 [32768, 16384], P('prow', 'pcol'), may hold values from -6 to 6
- sub_block: float32 [512, 512], replicated, may hold values from -0.25 to 0.25
- inv_first: float32 [512, 512], replicated, as said below
- inv_second: float32 [512, 512], replicated, as said below
Outputs:
- solved: float32 [2, 512, 16384], P(None, 'prow', 'pcol')
Inputs may be any that keep to these rules, and one draw needn't show every extreme that they name: inv_first is lower triangular with a positive diagonal. inv_second is lower triangular with a positive diagonal.
All inputs are finite; a program needn't handle non-finite values.
Results may differ from a plain program's by a relative error of at most 0.0003.
Values may be sent and summed in bfloat16 or wider, within the bound.
A program may use at most 64 MiB of HBM per device.

v0:
```python
import jax
import jax.numpy as jnp
from jax import lax
from jax.sharding import PartitionSpec as P


def mult(left, right):
    return jnp.dot(left, right, preferred_element_type=jnp.float32, precision=lax.Precision.HIGHEST)


def local(cross_cov, prev_rows, prev_solved, sub_block, inv_first, inv_second):
    terms = jnp.einsum(
        "kra,ac->krc",
        lax.all_gather(prev_rows, "pcol", axis=1, tiled=True),
        prev_solved,
        preferred_element_type=jnp.float32,
    )
    update = lax.psum_scatter(terms, "prow", scatter_dimension=1, tiled=True)
    first_part = cross_cov[0] - update[0]
    second_part = cross_cov[1] - update[1]
    local_rows = first_part.shape[0]
    offset = lax.axis_index("prow") * local_rows

    def own_rows(matrix):
        return lax.dynamic_slice_in_dim(matrix, offset, local_rows, 0)

    first_full = lax.all_gather(first_part, "prow", axis=0, tiled=True)
    solved_first = mult(own_rows(inv_first), first_full)
    solved_full = lax.all_gather(solved_first, "prow", axis=0, tiled=True)
    reduced = second_part - mult(own_rows(sub_block), solved_full)
    reduced_full = lax.all_gather(reduced, "prow", axis=0, tiled=True)
    solved_second = mult(own_rows(inv_second), reduced_full)
    return jnp.stack([solved_first, solved_second])


def solution(mesh):
    return jax.shard_map(
        local,
        mesh=mesh,
        in_specs=(
            P(None, "prow", "pcol"),
            P(None, "pcol", "prow"),
            P("prow", "pcol"),
            P(),
            P(),
            P(),
        ),
        out_specs=P(None, "prow", "pcol"),
        check_vma=False,
    )
```

profile of v0, /device:TPU:0, one launch (start us, length us, event | category | flops | bytes accessed | tf_op | source)
XLA Modules:
  0.0 230.7 jit_solution(13975077794349353256)
XLA Ops:
  6.5 0.0 copy-start
  6.5 0.0 all-gather.6.cloned.1.call-start
  6.5 0.7 all-gather.6.cloned.1.call-update
  7.3 0.0 reduce-scatter.2.cloned.1.call-start
  7.3 75.6 %all-gather.6.cloned.1.call-done = bf16[2,512,4096]{2,1,0:T(8,128)(2,1)} async-done(((bf16[2,32,4096]{2,1,0:T(8,128)(2,1)}), bf16[2,512,4096]{2,1,0:T(8,128)(2,1)}) %all-gather.6.cloned.1.call-update) | async-done | bytes 8388624 | tf_op jit(solution)/shard_map/all_gather | solution.py:14
  82.9 15.0 %fusion = f32[2,512,1024]{2,1,0:T(8,128)} fusion(bf16[2,512,4096]{2,1,0:T(8,128)(2,1)} %all-gather.6.cloned.1.call-done, bf16[4096,1024]{1,0:T(8,128)(2,1)} %param.8), kind=kOutput, calls=%fused_computation | convolution fusion | flops 8589934592 | bytes 20971520 | tf_op jit(solution)/shard_map/kra,ac->krc/dot_general | solution.py:12
  97.9 0.0 copy-start.2
  97.9 0.0 reduce-scatter.2.cloned.1.call-update
  98.0 0.0 all-gather.12.cloned.1.call-start
  98.0 37.6 %reduce-scatter.2.cloned.1.call-done = f32[2,64,1024]{2,1,0:T(8,128)} async-done(((f32[2,512,1024]{2,1,0:T(8,128)}), f32[2,64,1024]{2,1,0:T(8,128)}) %reduce-scatter.2.cloned.1.call-update) | async-done | bytes 524304 | tf_op jit(solution)/shard_map/reduce_scatter | solution.py:18
  135.6 0.0 copy-done.2
  135.6 0.0 copy-start.3
  135.6 1.8 slice_subtract_fusion.1
  137.3 0.0 all-gather.12.cloned.1.call-update
  137.4 0.0 all-gather.8.cloned.1.call-start
  137.4 24.1 %all-gather.12.cloned.1.call-done = f32[1,512,1024]{2,1,0:T(8,128)} async-done(((f32[1,64,1024]{2,1,0:T(8,128)}), f32[1,512,1024]{2,1,0:T(8,128)}) %all-gather.12.cloned.1.call-update) | async-done | bytes 2097168 | tf_op jit(solution)/shard_map/all_gather | solution.py:27
  161.5 0.0 copy-done
  161.5 3.7 %fusion.2 = f32[64,1024]{1,0:T(8,128)} fusion(f32[1,512,1024]{2,1,0:T(8,128)} %all-gather.12.cloned.1.call-done, f32[512,512]{1,0:T(8,128)S(1)} %copy-done, s32[]{:T(128)S(6)} %select_n.2), kind=kOutput, calls=%fused_computation.2 | convolution fusion | flops 402653184 | bytes 2490372 | tf_op jit(solution)/shard_map/dot_general | solution.py:8
  165.2 0.0 all-gather.8.cloned.1.call-update
  165.2 0.0 all-gather.10.cloned.1.call-start
  165.3 25.6 %all-gather.8.cloned.1.call-done = f32[512,1024]{1,0:T(8,128)} async-done(((f32[64,1024]{1,0:T(8,128)}), f32[512,1024]{1,0:T(8,128)}) %all-gather.8.cloned.1.call-update) | async-done | bytes 2097168 | tf_op jit(solution)/shard_map/all_gather | solution.py:29
  190.8 0.0 copy-done.3
  190.8 3.8 %convolution_subtract_fusion = f32[64,1024]{1,0:T(8,128)} fusion(f32[512,1024]{1,0:T(8,128)} %all-gather.8.cloned.1.call-done, f32[2,64,1024]{2,1,0:T(8,128)S(1)} %copy-done.3, f32[2,64,1024]{2,1,0:T(8,128)S(1)} %copy-done.2, f32[512,512]{1,0:T(8,128)} %param.9, s32[]{:T(128)S(6)} %select_n.2), kind=kOutput, calls=%fused_computation.4 | convolution fusion | flops 402784256 | bytes 3014660 | tf_op jit(solution)/shard_map/dot_general | solution.py:8
  194.6 0.0 copy-start.1
  194.6 0.0 all-gather.10.cloned.1.call-update
  194.6 25.6 %all-gather.10.cloned.1.call-done = f32[512,1024]{1,0:T(8,128)} async-done(((f32[64,1024]{1,0:T(8,128)}), f32[512,1024]{1,0:T(8,128)}) %all-gather.10.cloned.1.call-update) | async-done | bytes 2097168 | tf_op jit(solution)/shard_map/all_gather | solution.py:31
  220.2 3.0 %convolution_bitcast_fusion = f32[1,64,1024]{2,1,0:T(8,128)S(1)} fusion(f32[512,1024]{1,0:T(8,128)} %all-gather.10.cloned.1.call-done, f32[512,512]{1,0:T(8,128)} %param.11, s32[]{:T(128)S(6)} %select_n.2), kind=kOutput, calls=%fused_computation.5 | convolution fusion | flops 402653184 | bytes 2490372 | tf_op jit(solution)/shard_map/dot_general | solution.py:8
  223.3 0.0 copy-done.1
  223.3 0.8 pad_maximum_fusion
Async XLA Ops:
  6.5 155.0 %copy-start = (f32[512,512]{1,0:T(8,128)S(1)}, f32[512,512]{1,0:T(8,128)}, u32[]{:S(2)}) copy-start(f32[512,512]{1,0:T(8,128)} %param.10) | copy-start | bytes 3145732
  6.5 76.4 %all-gather.6.cloned.1.call-start = ((), (), s32[]{:S(2)}) async-start(), calls=%async_computation.1 | async-start | bytes 8912896 | tf_op jit(solution)/shard_map/all_gather | solution.py:14
  7.3 128.3 %reduce-scatter.2.cloned.1.call-start = ((), (), s32[]{:S(2)}) async-start(), calls=%async_computation.2 | async-start | bytes 4718592 | tf_op jit(solution)/shard_map/reduce_scatter | solution.py:18
  97.9 37.7 %copy-start.2 = (f32[2,64,1024]{2,1,0:T(8,128)S(1)}, f32[2,64,1024]{2,1,0:T(8,128)}, u32[]{:S(2)}) copy-start(f32[2,64,1024]{2,1,0:T(8,128)} %param.6) | copy-start | bytes 1572868
  98.0 63.5 %all-gather.12.cloned.1.call-start = ((), (), s32[]{:S(2)}) async-start(), calls=%async_computation.5 | async-start | bytes 2359296 | tf_op jit(solution)/shard_map/all_gather | solution.py:27
  135.6 55.2 %copy-start.3 = (f32[2,64,1024]{2,1,0:T(8,128)S(1)}, f32[2,64,1024]{2,1,0:T(8,128)}, u32[]{:S(2)}) copy-start(f32[2,64,1024]{2,1,0:T(8,128)} %reduce-scatter.2.cloned.1.call-done) | copy-start | bytes 1572868
  137.4 53.5 %all-gather.8.cloned.1.call-start = ((), (), s32[]{:S(2)}) async-start(), calls=%async_computation.3 | async-start | bytes 2359296 | tf_op jit(solution)/shard_map/all_gather | solution.py:29
  165.2 55.0 %all-gather.10.cloned.1.call-start = ((), (), s32[]{:S(2)}) async-start(), calls=%async_computation.4 | async-start | bytes 2359296 | tf_op jit(solution)/shard_map/all_gather | solution.py:31
  194.6 28.7 %copy-start.1 = (f32[64,1024]{1,0:T(8,128)S(1)}, f32[64,1024]{1,0:T(8,128)}, u32[]{:S(2)}) copy-start(f32[64,1024]{1,0:T(8,128)} %fusion.2) | copy-start | bytes 786436
Sparse Core Ops, SparseCore 0:
  9.6 73.3 all-gather.5
  98.1 37.4 reduce-scatter.1
  137.5 23.9 all-gather.11
  165.3 25.4 all-gather.7
  194.8 25.4 all-gather.9
where the time goes:
time: 232 us; the launch traced here: 231 us
  waiting for transfers between devices  189 us (81%)
  matrix products  25.5 us (11%)
  between operations  13.2 us (6%)
  other arithmetic  2.59 us (1%)
    all_gather x1, waiting for transfers between devices, local(): lax.all_gather(prev_rows, 'pcol', axis=1, tiled=True)  75.6 us
    reduce_scatter x1, waiting for transfers between devices, local(): update = lax.psum_scatter(terms, 'prow', scatter_dimension=1, tiled=True)  37.6 us
    all_gather x1, waiting for transfers between devices, local(): reduced_full = lax.all_gather(reduced, 'prow', axis=0, tiled=True)  25.6 us
    all_gather x1, waiting for transfers between devices, local(): solved_full = lax.all_gather(solved_first, 'prow', axis=0, tiled=True)  25.6 us
    all_gather x1, waiting for transfers between devices, local(): first_full = lax.all_gather(first_part, 'prow', axis=0, tiled=True)  24.1 us
    dot_general x1, matrix products, local(): jnp.einsum('kra,ac->krc', lax.all_gather(prev_rows, 'pcol', axis=1, tiled...  15 us
    dot_general x3, matrix products, mult(): jnp.dot(left, right, preferred_element_type=jnp.float32, precision=lax.Pr...  10.5 us
  transfers between devices with their start and end apart: 5, of which 5 were waited for; matrix products, arithmetic and copies ran while one was open for 0% of the time, Pallas kernels for 0%

commit v1 on v0

v1 whole, which is shorter than its diff:
```python
import jax
import jax.numpy as jnp
from jax import lax
from jax.sharding import PartitionSpec as P


def mult(left, right, precision=lax.Precision.HIGHEST):
    return jnp.dot(left, right, preferred_element_type=jnp.float32, precision=precision)


def local(cross_cov, prev_rows, prev_solved, sub_block, inv_first, inv_second):
    rows = cross_cov.shape[1]
    terms = jnp.einsum(
        "kra,ac->krc",
        lax.all_gather(prev_rows, "pcol", axis=1, tiled=True),
        prev_solved,
        preferred_element_type=jnp.float32,
    )
    offset = lax.axis_index("prow") * rows
    rhs = lax.dynamic_update_slice_in_dim(-terms, lax.dynamic_slice_in_dim(-terms, offset, rows, 1) + cross_cov, offset, 1)
    coupling = -mult(inv_second, mult(sub_block, inv_first))
    high = lax.Precision.HIGH
    nb = inv_first.shape[0]
    transform = jnp.concatenate([
        jnp.concatenate([inv_first, jnp.zeros_like(inv_first)], axis=1),
        jnp.concatenate([coupling, inv_second], axis=1),
    ])
    both = mult(transform, rhs.reshape(2 * nb, -1), high).reshape(rhs.shape)
    return lax.psum_scatter(both, "prow", scatter_dimension=1, tiled=True)


def solution(mesh):
    return jax.shard_map(
        local,
        mesh=mesh,
        in_specs=(
            P(None, "prow", "pcol"),
            P(None, "pcol", "prow"),
            P("prow", "pcol"),
            P(),
            P(),
            P(),
        ),
        out_specs=P(None, "prow", "pcol"),
        check_vma=False,
    )
```

time: 232 us -> 149 us (0.64)
  waiting for transfers between devices: 189 us -> 95.3 us
  local copies, waits for them, and re-layouts: 0.02 us -> 10.9 us
    all_gather x3 -> x0, waiting for transfers between devices: 75.3 us -> none  [the longest x1 25.6 us: local(): reduced_full = lax.all_gather(reduced, 'prow', axis=0, tiled=True)]
    all_gather x1, waiting for transfers between devices: 75.6 us -> 57 us  [local(): lax.all_gather(prev_rows, 'pcol', axis=1, tiled=True)]
    dot_general x0 -> x1, local copies, waits for them, and re-layouts: none -> 5.55 us  [mult(): jnp.dot(left, right, preferred_element_type=jnp.float32, precision=precis...]
    unnamed x8 -> x16, local copies, waits for them, and re-layouts: 0.02 us -> 5.34 us
    dot_general x3, matrix products: 10.5 us -> 13.6 us  [mult(): jnp.dot(left, right, preferred_element_type=jnp.float32, precision=precis...]
    concatenate x0 -> x1, other arithmetic: none -> 2.35 us  [local(): jnp.concatenate([jnp.concatenate([inv_first, jnp.zeros_like(inv_first)],...]
  transfers between devices with their start and end apart: 5 -> 2, of which waited for: 5 -> 2; matrix products, arithmetic and copies ran while one was open for 0% -> 12% of each run, Pallas kernels for 0% -> 0%
where the time goes in v1:
time: 149 us
  waiting for transfers between devices  95.3 us (64%)
  matrix products  26.9 us (18%)
  between operations  13.5 us (9%)
  local copies, waits for them, and re-layouts  10.9 us (7%)
  other arithmetic  2.47 us (2%)
    all_gather x1, waiting for transfers between devices, local(): lax.all_gather(prev_rows, 'pcol', axis=1, tiled=True)  57 us
    reduce_scatter x1, waiting for transfers between devices, local(): return lax.psum_scatter(both, 'prow', scatter_dimension=1, tiled=True)  37.6 us
    dot_general x3, matrix products, mult(): jnp.dot(left, right, preferred_element_type=jnp.float32, precision=precis...  13.6 us
    dot_general x1, matrix products, local(): jnp.einsum('kra,ac->krc', lax.all_gather(prev_rows, 'pcol', axis=1, tiled...  13.2 us
    dot_general x1, local copies, waits for them, and re-layouts, mult(): jnp.dot(left, right, preferred_element_type=jnp.float32, precision=precis...  5.55 us
    unnamed x16, local copies, waits for them, and re-layouts  5.34 us
  transfers between devices with their start and end apart: 2, of which 2 were waited for; matrix products, arithmetic and copies ran while one was open for 12% of the time, Pallas kernels for 0%

profile of v1, /device:TPU:0, one launch (start us, length us, event | category | flops | bytes accessed | tf_op | source)
XLA Modules:
  0.0 149.0 jit_solution(13113632251256436975)
XLA Ops:
  6.5 0.0 copy-start
  6.5 0.0 copy-start.1
  6.5 0.0 copy-start.2
  6.5 0.0 all-gather.2.cloned.1.call-start
  6.5 0.7 all-gather.2.cloned.1.call-update
  7.3 0.0 reduce-scatter.2.cloned.1.call-start
  7.3 2.8 %copy.7 = f32[512,512]{0,1:T(8,128)} copy(f32[512,512]{1,0:T(8,128)} %param.10) | data formatting | bytes 2097152 | tf_op args[4]
  10.1 2.5 %copy.8 = f32[512,512]{0,1:T(8,128)} copy(f32[512,512]{1,0:T(8,128)} %param.11) | data formatting | bytes 2097152 | tf_op args[5]
  12.6 0.0 copy-done
  12.6 0.0 copy-done.1
  12.6 0.0 copy-start.3
  12.6 0.0 copy-start.4
  12.6 1.9 %fusion.6 = f32[512,512]{1,0:T(8,128)S(1)} fusion(f32[512,512]{1,0:T(8,128)S(1)} %copy-done, f32[512,512]{1,0:T(8,128)S(1)} %copy-done.1), kind=kOutput, calls=%fused_computation.8 | convolution fusion | flops 1610612736 | bytes 3145728 | tf_op jit(solution)/shard_map/dot_general | solution.py:8
  14.5 0.0 copy-done.2
  14.5 3.5 %fusion.5 = f32[512,512]{0,1:T(8,128)S(1)} fusion(f32[512,512]{1,0:T(8,128)S(1)} %fusion.6, f32[512,512]{1,0:T(8,128)S(1)} %copy-done.2), kind=kOutput, calls=%fused_computation.6 | convolution fusion | flops 1610874880 | bytes 3145728 | tf_op jit(solution)/shard_map/dot_general | solution.py:8
  18.0 0.0 copy-done.3
  18.0 0.0 copy-done.4
  18.0 2.4 %select_maximum_fusion = f32[1024,1024]{0,1:T(8,128)} fusion(f32[512,512]{0,1:T(8,128)S(1)} %copy-done.3, f32[512,512]{0,1:T(8,128)S(1)} %copy-done.4, f32[512,512]{0,1:T(8,128)S(1)} %fusion.5), kind=kLoop, calls=%fused_computation.2 | loop fusion | flops 4194304 | bytes 7340032 | tf_op jit(solution)/shard_map/concatenate | solution.py:24
  20.4 5.5 %copy.10 = f32[1024,1024]{1,0:T(8,128)} copy(f32[1024,1024]{0,1:T(8,128)} %select_maximum_fusion) | data formatting | bytes 8388608 | tf_op jit(solution)/shard_map/dot_general | solution.py:8
  25.9 0.0 copy-start.6
  25.9 57.0 %all-gather.2.cloned.1.call-done = bf16[2,512,4096]{2,1,0:T(8,128)(2,1)} async-done(((bf16[2,32,4096]{2,1,0:T(8,128)(2,1)}), bf16[2,512,4096]{2,1,0:T(8,128)(2,1)}) %all-gather.2.cloned.1.call-update) | async-done | bytes 8388624 | tf_op jit(solution)/shard_map/all_gather | solution.py:15
  82.9 0.0 copy-start.5
  82.9 13.2 %fusion.2 = f32[2,512,1024]{2,1,0:T(8,128)S(1)} fusion(bf16[2,512,4096]{2,1,0:T(8,128)(2,1)} %all-gather.2.cloned.1.call-done, bf16[4096,1024]{1,0:T(8,128)(2,1)} %param.8), kind=kOutput, calls=%fused_computation.4 | convolution fusion | flops 8590983168 | bytes 20971520 | tf_op jit(solution)/shard_map/kra,ac->krc/dot_general | solution.py:13
  96.2 0.0 copy-done.6
  96.2 0.1 add_dynamic-update-slice_fusion
  96.3 0.0 copy-done.5
  96.3 8.3 %fusion.7 = f32[2,512,1024]{2,1,0:T(8,128)} fusion(f32[2,512,1024]{2,1,0:T(8,128)S(1)} %bitcast.18, f32[1024,1024,1]{1,0,2:T(8,128)S(1)} %bitcast.19), kind=kOutput, calls=%fused_computation.9 | convolution fusion | flops 6442450944 | bytes 12582912 | tf_op jit(solution)/shard_map/dot_general | solution.py:8
  104.6 0.0 reduce-scatter.2.cloned.1.call-update
  104.6 37.6 %reduce-scatter.2.cloned.1.call-done = f32[2,64,1024]{2,1,0:T(8,128)} async-done(((f32[2,512,1024]{2,1,0:T(8,128)}), f32[2,64,1024]{2,1,0:T(8,128)}) %reduce-scatter.2.cloned.1.call-update) | async-done | bytes 524304 | tf_op jit(solution)/shard_map/reduce_scatter | solution.py:29
Async XLA Ops:
  6.5 6.1 %copy-start = (f32[512,512]{1,0:T(8,128)S(1)}, f32[512,512]{1,0:T(8,128)}, u32[]{:S(2)}) copy-start(f32[512,512]{1,0:T(8,128)} %param.9) | copy-start | bytes 3145732
  6.5 6.1 %copy-start.1 = (f32[512,512]{1,0:T(8,128)S(1)}, f32[512,512]{1,0:T(8,128)}, u32[]{:S(2)}) copy-start(f32[512,512]{1,0:T(8,128)} %param.10) | copy-start | bytes 3145732
  6.5 8.0 %copy-start.2 = (f32[512,512]{1,0:T(8,128)S(1)}, f32[512,512]{1,0:T(8,128)}, u32[]{:S(2)}) copy-start(f32[512,512]{1,0:T(8,128)} %param.11) | copy-start | bytes 3145732
  6.5 76.4 %all-gather.2.cloned.1.call-start = ((), (), s32[]{:S(2)}) async-start(), calls=%async_computation.1 | async-start | bytes 8912896 | tf_op jit(solution)/shard_map/all_gather | solution.py:15
  7.3 134.9 %reduce-scatter.2.cloned.1.call-start = ((), (), s32[]{:S(2)}) async-start(), calls=%async_computation.2 | async-start | bytes 4718592 | tf_op jit(solution)/shard_map/reduce_scatter | solution.py:29
  12.6 5.4 %copy-start.3 = (f32[512,512]{0,1:T(8,128)S(1)}, f32[512,512]{0,1:T(8,128)}, u32[]{:S(2)}) copy-start(f32[512,512]{0,1:T(8,128)} %copy.7) | copy-start | bytes 3145732
  12.6 5.4 %copy-start.4 = (f32[512,512]{0,1:T(8,128)S(1)}, f32[512,512]{0,1:T(8,128)}, u32[]{:S(2)}) copy-start(f32[512,512]{0,1:T(8,128)} %copy.8) | copy-start | bytes 3145732
  25.9 70.3 %copy-start.6 = (f32[2,64,1024]{2,1,0:T(8,128)S(1)}, f32[2,64,1024]{2,1,0:T(8,128)}, u32[]{:S(2)}) copy-start(f32[2,64,1024]{2,1,0:T(8,128)} %param.6) | copy-start | bytes 1572868
  82.9 13.4 %copy-start.5 = (f32[1024,1024]{1,0:T(8,128)S(1)}, f32[1024,1024]{1,0:T(8,128)}, u32[]{:S(2)}) copy-start(f32[1024,1024]{1,0:T(8,128)} %copy.10) | copy-start | bytes 12582916
Sparse Core Ops, SparseCore 0:
  9.6 73.3 all-gather.1
  104.8 37.4 reduce-scatter.1

commit v2 on v1

--- a/solution.py
+++ b/solution.py
@@ -10,12 +10,14 @@
 
 def local(cross_cov, prev_rows, prev_solved, sub_block, inv_first, inv_second):
     rows = cross_cov.shape[1]
-    terms = jnp.einsum(
-        "kra,ac->krc",
-        lax.all_gather(prev_rows, "pcol", axis=1, tiled=True),
-        prev_solved,
-        preferred_element_type=jnp.float32,
-    )
+    pieces = 2
+    width = prev_rows.shape[2] // pieces
+    terms = None
+    for p in range(pieces):
+        gathered = lax.all_gather(prev_rows[:, :, p * width:(p + 1) * width], "pcol", axis=1, tiled=True)
+        part = jnp.einsum("kra,ac->krc", gathered, prev_solved[p * width:(p + 1) * width],
+                          preferred_element_type=jnp.float32)
+        terms = part if terms is None else terms + part
     offset = lax.axis_index("prow") * rows
     rhs = lax.dynamic_update_slice_in_dim(-terms, lax.dynamic_slice_in_dim(-terms, offset, rows, 1) + cross_cov, offset, 1)
     coupling = -mult(inv_second, mult(sub_block, inv_first))
@@ -25,8 +27,13 @@
         jnp.concatenate([inv_first, jnp.zeros_like(inv_first)], axis=1),
         jnp.concatenate([coupling, inv_second], axis=1),
     ])
-    both = mult(transform, rhs.reshape(2 * nb, -1), high).reshape(rhs.shape)
-    return lax.psum_scatter(both, "prow", scatter_dimension=1, tiled=True)
+    flat = rhs.reshape(2 * nb, -1)
+    cols = flat.shape[1] // pieces
+    out = []
+    for p in range(pieces):
+        both = mult(transform, flat[:, p * cols:(p + 1) * cols], high).reshape(2, nb, cols)
+        out.append(lax.psum_scatter(both, "prow", scatter_dimension=1, tiled=True))
+    return jnp.concatenate(out, axis=2)
 
 
 def solution(mesh):

time: 149 us -> 208 us (1.40)
  waiting for transfers between devices: 95.3 us -> 151 us
  matrix products: 26.9 us -> 36.3 us
  local copies, waits for them, and re-layouts: 10.9 us -> 6 us
    all_gather x1 -> x2, waiting for transfers between devices: 57 us -> 88.6 us  [local(): lax.all_gather(prev_rows[:, :, p * width:(p + 1) * width], 'pcol', axis=1...]
    reduce_scatter x1 -> x2, waiting for transfers between devices: 37.6 us -> 61.2 us  [local(): out.append(lax.psum_scatter(both, 'prow', scatter_dimension=1, tiled=True))]
    dot_general x1 -> x2, matrix products: 13.2 us -> 19.2 us  [local(): jnp.einsum('kra,ac->krc', gathered, prev_solved[p * width:(p + 1) * width...]
    dot_general x1 -> x0, local copies, waits for them, and re-layouts: 5.55 us -> none  [mult(): jnp.dot(left, right, preferred_element_type=jnp.float32, precision=precis...]
    dot_general x3 -> x4, matrix products: 13.6 us -> 17.1 us  [mult(): jnp.dot(left, right, preferred_element_type=jnp.float32, precision=precis...]
  transfers between devices with their start and end apart: 2 -> 4, of which waited for: 2 -> 4; matrix products, arithmetic and copies ran while one was open for 12% -> 12% of each run, Pallas kernels for 0% -> 0%
where the time goes in v2:
time: 208 us
  waiting for transfers between devices  151 us (73%)
  matrix products  36.3 us (17%)
  between operations  13.2 us (6%)
  local copies, waits for them, and re-layouts  6 us (3%)
    all_gather x2, waiting for transfers between devices, local(): lax.all_gather(prev_rows[:, :, p * width:(p + 1) * width], 'pcol', axis=1...  88.6 us
    reduce_scatter x2, waiting for transfers between devices, local(): out.append(lax.psum_scatter(both, 'prow', scatter_dimension=1, tiled=True))  61.2 us
    dot_general x2, matrix products, local(): jnp.einsum('kra,ac->krc', gathered, prev_solved[p * width:(p + 1) * width...  19.2 us
    dot_general x4, matrix products, mult(): jnp.dot(left, right, preferred_element_type=jnp.float32, precision=precis...  17.1 us
  transfers between devices with their start and end apart: 4, of which 4 were waited for; matrix products, arithmetic and copies ran while one was open for 12% of the time, Pallas kernels for 0%

profile of v2, /device:TPU:0, one launch (start us, length us, event | category | flops | bytes accessed | tf_op | source)
XLA Modules:
  0.0 208.2 jit_solution(16049799425421940616)
XLA Ops:
  6.5 0.0 copy-start
  6.5 0.0 all-gather.5.cloned.1.call-start
  6.5 2.0 fusion.23
  8.6 0.0 all-gather.5.cloned.1.call-update
  8.6 0.0 all-gather.3.cloned.1.call-start
  8.7 0.7 all-gather.3.cloned.1.call-update
  9.4 0.0 reduce-scatter.5.cloned.1.call-start
  9.4 2.5 %copy.7 = f32[512,512]{0,1:T(8,128)} copy(f32[512,512]{1,0:T(8,128)} %param.10) | data formatting | bytes 2097152 | tf_op args[4]
  12.0 0.0 copy-done.2
  12.0 1.4 copy.8
  13.4 0.0 copy-done
  13.4 0.0 copy-done.1
  13.4 1.9 fusion.24
  15.2 3.5 %fusion.16 = f32[512,512]{0,1:T(8,128)S(1)} fusion(f32[512,512]{1,0:T(8,128)S(1)} %fusion.24, f32[512,512]{1,0:T(8,128)S(1)} %copy-done.2), kind=kOutput, calls=%fused_computation.18 | convolution fusion | flops 1610874880 | bytes 3145728 | tf_op jit(solution)/shard_map/dot_general | solution.py:8
  18.7 45.1 %all-gather.5.cloned.1.call-done = bf16[2,512,2048]{2,1,0:T(8,128)(2,1)} async-done(((bf16[2,32,2048]{2,1,0:T(8,128)(2,1)}), bf16[2,512,2048]{2,1,0:T(8,128)(2,1)}) %all-gather.5.cloned.1.call-update) | async-done | bytes 4194320 | tf_op jit(solution)/shard_map/all_gather | solution.py:17
  63.8 9.9 %fusion = f32[2,512,1024]{2,1,0:T(8,128)} fusion(bf16[2,512,2048]{2,1,0:T(8,128)(2,1)} %all-gather.5.cloned.1.call-done, bf16[4096,1024]{1,0:T(8,128)(2,1)} %param.8), kind=kOutput, calls=%fused_computation.2 | convolution fusion | flops 4294967296 | bytes 12582912 | tf_op jit(solution)/shard_map/kra,ac->krc/dot_general | solution.py:18
  73.7 43.6 %all-gather.3.cloned.1.call-done = bf16[2,512,2048]{2,1,0:T(8,128)(2,1)} async-done(((bf16[2,32,2048]{2,1,0:T(8,128)(2,1)}), bf16[2,512,2048]{2,1,0:T(8,128)(2,1)}) %all-gather.3.cloned.1.call-update) | async-done | bytes 4194320 | tf_op jit(solution)/shard_map/all_gather | solution.py:17
  117.3 9.2 %add_negate_fusion = f32[2,512,1024]{2,1,0:T(8,128)S(1)} fusion(f32[2,512,1024]{2,1,0:T(8,128)} %fusion, bf16[2,512,2048]{2,1,0:T(8,128)(2,1)} %all-gather.3.cloned.1.call-done, bf16[4096,1024]{1,0:T(8,128)(2,1)} %param.8), kind=kOutput, calls=%fused_computation.6 | convolution fusion | flops 4297064448 | bytes 16777216 | tf_op jit(solution)/shard_map/kra,ac->krc/dot_general | solution.py:18
  126.5 0.0 copy-done.5
  126.5 0.1 add_dynamic-update-slice_fusion
  126.6 0.0 copy-start.6
  126.6 0.0 copy-done.3
  126.7 0.0 copy-done.4
  126.7 5.1 %fusion.6 = f32[1024,512]{1,0:T(8,128)} fusion(f32[512,512]{0,1:T(8,128)S(1)} %copy-done.3, f32[512,512]{0,1:T(8,128)S(1)} %copy-done.4, f32[512,512]{0,1:T(8,128)S(1)} %fusion.16, f32[1024,1024]{1,0:T(8,128)S(1)} %bitcast.21), kind=kOutput, calls=%fused_computation.9 | convolution fusion | flops 3225419776 | bytes 7340032 | tf_op jit(solution)/shard_map/dot_general | solution.py:8
  131.7 0.0 copy-done.6
  131.8 0.0 reduce-scatter.5.cloned.1.call-update
  131.8 0.0 reduce-scatter.3.cloned.1.call-start
  131.8 6.7 %fusion.7 = f32[1024,512]{1,0:T(8,128)} fusion(f32[512,512]{0,1:T(8,128)S(1)} %copy-done.3, f32[512,512]{0,1:T(8,128)} %copy.8, f32[512,512]{0,1:T(8,128)S(1)} %fusion.16, f32[1024,1024]{1,0:T(8,128)} %bitcast.22), kind=kOutput, calls=%fused_computation.10 | convolution fusion | flops 3225419776 | bytes 7340032 | tf_op jit(solution)/shard_map/dot_general | solution.py:8
  138.6 0.0 reduce-scatter.3.cloned.1.call-update
  138.6 26.6 %reduce-scatter.5.cloned.1.call-done = f32[2,64,512]{2,1,0:T(8,128)} async-done(((f32[2,512,512]{2,1,0:T(8,128)}), f32[2,64,512]{2,1,0:T(8,128)}) %reduce-scatter.5.cloned.1.call-update) | async-done | bytes 262160 | tf_op jit(solution)/shard_map/reduce_scatter | solution.py:35
  165.2 34.7 %reduce-scatter.3.cloned.1.call-done = f32[2,64,512]{2,1,0:T(8,128)} async-done(((f32[2,512,512]{2,1,0:T(8,128)}), f32[2,64,512]{2,1,0:T(8,128)}) %reduce-scatter.3.cloned.1.call-update) | async-done | bytes 262160 | tf_op jit(solution)/shard_map/reduce_scatter | solution.py:35
  199.8 1.9 pad_maximum_fusion
  (5 shorter events, 0.0 us)
Async XLA Ops:
  6.5 6.8 %copy-start = (f32[512,512]{1,0:T(8,128)S(1)}, f32[512,512]{1,0:T(8,128)}, u32[]{:S(2)}) copy-start(f32[512,512]{1,0:T(8,128)} %param.9) | copy-start | bytes 3145732
  6.5 6.8 %copy-start.1 = (f32[512,512]{1,0:T(8,128)S(1)}, f32[512,512]{1,0:T(8,128)}, u32[]{:S(2)}) copy-start(f32[512,512]{1,0:T(8,128)} %param.10) | copy-start | bytes 3145732
  6.5 5.4 %copy-start.2 = (f32[512,512]{1,0:T(8,128)S(1)}, f32[512,512]{1,0:T(8,128)}, u32[]{:S(2)}) copy-start(f32[512,512]{1,0:T(8,128)} %param.11) | copy-start | bytes 3145732
  6.5 57.2 %all-gather.5.cloned.1.call-start = ((), (), s32[]{:S(2)}) async-start(), calls=%async_computation.3 | async-start | bytes 4456448 | tf_op jit(solution)/shard_map/all_gather | solution.py:17
  8.6 108.6 %all-gather.3.cloned.1.call-start = ((), (), s32[]{:S(2)}) async-start(), calls=%async_computation.2 | async-start | bytes 4456448 | tf_op jit(solution)/shard_map/all_gather | solution.py:17
  9.4 155.8 %reduce-scatter.5.cloned.1.call-start = ((), (), s32[]{:S(2)}) async-start(), calls=%async_computation.5 | async-start | bytes 2359296 | tf_op jit(solution)/shard_map/reduce_scatter | solution.py:35
  73.7 53.0 %copy-start.3 = (f32[512,512]{0,1:T(8,128)S(1)}, f32[512,512]{0,1:T(8,128)}, u32[]{:S(2)}) copy-start(f32[512,512]{0,1:T(8,128)} %copy.7) | copy-start | bytes 3145732
  117.3 9.3 %copy-start.5 = (f32[2,64,1024]{2,1,0:T(8,128)S(1)}, f32[2,64,1024]{2,1,0:T(8,128)}, u32[]{:S(2)}) copy-start(f32[2,64,1024]{2,1,0:T(8,128)} %param.6) | copy-start | bytes 1572868
  117.3 9.4 %copy-start.4 = (f32[512,512]{0,1:T(8,128)S(1)}, f32[512,512]{0,1:T(8,128)}, u32[]{:S(2)}) copy-start(f32[512,512]{0,1:T(8,128)} %copy.8) | copy-start | bytes 3145732
  126.6 5.1 %copy-start.6 = (f32[2,512,1024]{2,1,0:T(8,128)}, f32[2,512,1024]{2,1,0:T(8,128)S(1)}, u32[]{:S(2)}) copy-start(f32[2,512,1024]{2,1,0:T(8,128)S(1)} %add_dynamic-update-slice_fusion) | copy-start | bytes 12582916
  131.8 68.1 %reduce-scatter.3.cloned.1.call-start = ((), (), s32[]{:S(2)}) async-start(), calls=%async_computation.4 | async-start | bytes 2359296 | tf_op jit(solution)/shard_map/reduce_scatter | solution.py:35
Sparse Core Ops, SparseCore 0:
  9.6 54.1 all-gather.4
  66.0 51.2 all-gather.2
  131.9 33.2 reduce-scatter.4
  167.4 32.3 reduce-scatter.2

commit v3 on v1

v3 whole, which is shorter than its diff:
```python
import jax
import jax.numpy as jnp
from jax import lax
from jax.sharding import PartitionSpec as P


def mult(left, right):
    return jnp.dot(left, right, preferred_element_type=jnp.float32, precision=lax.Precision.HIGH)


def local(cross_cov, prev_rows, prev_solved, sub_block, inv_first, inv_second):
    rows = cross_cov.shape[1]
    terms = jnp.einsum(
        "kra,ac->krc",
        lax.all_gather(prev_rows, "pcol", axis=1, tiled=True),
        prev_solved,
        preferred_element_type=jnp.float32,
    )
    offset = lax.axis_index("prow") * rows
    rhs = lax.dynamic_update_slice_in_dim(-terms, lax.dynamic_slice_in_dim(-terms, offset, rows, 1) + cross_cov, offset, 1)
    first = mult(inv_first, rhs[0])
    second = mult(inv_second, rhs[1] - mult(sub_block, first))
    both = jnp.concatenate([first, second]).reshape((2,) + first.shape)
    return lax.psum_scatter(both, "prow", scatter_dimension=1, tiled=True)


def solution(mesh):
    return jax.shard_map(
        local,
        mesh=mesh,
        in_specs=(
            P(None, "prow", "pcol"),
            P(None, "pcol", "prow"),
            P("prow", "pcol"),
            P(),
            P(),
            P(),
        ),
        out_specs=P(None, "prow", "pcol"),
        check_vma=False,
    )
```

time: 149 us -> 149 us (level)
  waiting for transfers between devices: 95.3 us -> 114 us
  local copies, waits for them, and re-layouts: 10.9 us -> 0.02 us
  matrix products: 26.9 us -> 18.7 us
    all_gather x1, waiting for transfers between devices: 57 us -> 75.6 us  [local(): lax.all_gather(prev_rows, 'pcol', axis=1, tiled=True)]
    dot_general x3, matrix products: 13.6 us -> 5.64 us  [mult(): jnp.dot(left, right, preferred_element_type=jnp.float32, precision=lax.Pr...]
    dot_general x1 -> x0, local copies, waits for them, and re-layouts: 5.55 us -> none  [mult(): jnp.dot(left, right, preferred_element_type=jnp.float32, precision=precis...]
    unnamed x16 -> x8, local copies, waits for them, and re-layouts: 5.34 us -> 0.02 us
  transfers between devices with their start and end apart: 2 -> 2, of which waited for: 2 -> 2; matrix products, arithmetic and copies ran while one was open for 12% -> 0% of each run, Pallas kernels for 0% -> 0%
where the time goes in v3:
time: 149 us
  waiting for transfers between devices  114 us (77%)
  matrix products  18.7 us (13%)
  between operations  13.5 us (9%)
  other arithmetic  2.58 us (2%)
    all_gather x1, waiting for transfers between devices, local(): lax.all_gather(prev_rows, 'pcol', axis=1, tiled=True)  75.6 us
    reduce_scatter x1, waiting for transfers between devices, local(): return lax.psum_scatter(both, 'prow', scatter_dimension=1, tiled=True)  37.5 us
    dot_general x1, matrix products, local(): jnp.einsum('kra,ac->krc', lax.all_gather(prev_rows, 'pcol', axis=1, tiled...  13.1 us
    dot_general x3, matrix products, mult(): jnp.dot(left, right, preferred_element_type=jnp.float32, precision=lax.Pr...  5.64 us
  transfers between devices with their start and end apart: 2, of which 2 were waited for; matrix products, arithmetic and copies ran while one was open for 0% of the time, Pallas kernels for 0%

profile of v3, /device:TPU:0, one launch (start us, length us, event | category | flops | bytes accessed | tf_op | source)
XLA Modules:
  0.0 148.7 jit_solution(808641312518555056)
XLA Ops:
  6.5 0.0 copy-start
  6.5 0.0 all-gather.2.cloned.1.call-start
  6.5 0.7 all-gather.2.cloned.1.call-update
  7.3 0.0 reduce-scatter.2.cloned.1.call-start
  7.3 0.0 copy-start.3
  7.3 75.6 %all-gather.2.cloned.1.call-done = bf16[2,512,4096]{2,1,0:T(8,128)(2,1)} async-done(((bf16[2,32,4096]{2,1,0:T(8,128)(2,1)}), bf16[2,512,4096]{2,1,0:T(8,128)(2,1)}) %all-gather.2.cloned.1.call-update) | async-done | bytes 8388624 | tf_op jit(solution)/shard_map/all_gather | solution.py:15
  82.9 13.1 %fusion.2 = f32[2,512,1024]{2,1,0:T(8,128)S(1)} fusion(bf16[2,512,4096]{2,1,0:T(8,128)(2,1)} %all-gather.2.cloned.1.call-done, bf16[4096,1024]{1,0:T(8,128)(2,1)} %param.8), kind=kOutput, calls=%fused_computation.3 | convolution fusion | flops 8590983168 | bytes 20971520 | tf_op jit(solution)/shard_map/kra,ac->krc/dot_general | solution.py:13
  96.0 0.0 copy-done.3
  96.0 0.0 copy-start.1
  96.0 0.1 add_dynamic-update-slice_fusion
  96.2 0.0 copy-done
  96.2 0.0 copy-start.2
  96.2 1.9 %fusion.8 = f32[1024,512]{0,1:T(8,128)S(1)} fusion(f32[512,512]{1,0:T(8,128)S(1)} %copy-done, f32[2,512,1024]{2,1,0:T(8,128)S(1)} %add_dynamic-update-slice_fusion), kind=kOutput, calls=%fused_computation.8 | convolution fusion | flops 1610612736 | bytes 5242880 | tf_op jit(solution)/shard_map/dot_general | solution.py:8
  98.0 0.0 copy-done.1
  98.1 1.9 %fusion.13 = f32[1024,512]{0,1:T(8,128)S(1)} fusion(f32[1024,512]{0,1:T(8,128)S(1)} %fusion.8, f32[512,512]{1,0:T(8,128)S(1)} %copy-done.1), kind=kOutput, calls=%fused_computation.12 | convolution fusion | flops 1610612736 | bytes 5242880 | tf_op jit(solution)/shard_map/dot_general | solution.py:8
  100.0 0.0 copy-done.2
  100.0 1.9 %fusion.10 = f32[512,1024]{1,0:T(8,128)S(1)} fusion(f32[512,512]{1,0:T(8,128)S(1)} %copy-done.2, f32[2,512,1024]{2,1,0:T(8,128)S(1)} %add_dynamic-update-slice_fusion, f32[1024,512]{0,1:T(8,128)S(1)} %fusion.13), kind=kOutput, calls=%fused_computation.10 | convolution fusion | flops 1611137024 | bytes 7340032 | tf_op jit(solution)/shard_map/dot_general | solution.py:8
  101.9 2.5 %pad_maximum_fusion = f32[1024,1024]{1,0:T(8,128)} fusion(f32[512,1024]{1,0:T(8,128)S(1)} %fusion.10, f32[512,1024]{1,0:T(8,128)S(1)} %bitcast.31), kind=kLoop, calls=%fused_computation.2 | loop fusion | flops 1048576 | bytes 8388608 | tf_op jit(solution)/shard_map/concatenate | solution.py:23
  104.3 0.0 reduce-scatter.2.cloned.1.call-update
  104.4 37.5 %reduce-scatter.2.cloned.1.call-done = f32[2,64,1024]{2,1,0:T(8,128)} async-done(((f32[2,512,1024]{2,1,0:T(8,128)}), f32[2,64,1024]{2,1,0:T(8,128)}) %reduce-scatter.2.cloned.1.call-update) | async-done | bytes 524304 | tf_op jit(solution)/shard_map/reduce_scatter | solution.py:24
Async XLA Ops:
  6.5 89.6 %copy-start = (f32[512,512]{1,0:T(8,128)S(1)}, f32[512,512]{1,0:T(8,128)}, u32[]{:S(2)}) copy-start(f32[512,512]{1,0:T(8,128)} %param.10) | copy-start | bytes 3145732
  6.5 76.4 %all-gather.2.cloned.1.call-start = ((), (), s32[]{:S(2)}) async-start(), calls=%async_computation.1 | async-start | bytes 8912896 | tf_op jit(solution)/shard_map/all_gather | solution.py:15
  7.3 134.6 %reduce-scatter.2.cloned.1.call-start = ((), (), s32[]{:S(2)}) async-start(), calls=%async_computation.2 | async-start | bytes 4718592 | tf_op jit(solution)/shard_map/reduce_scatter | solution.py:24
  7.3 88.7 %copy-start.3 = (f32[2,64,1024]{2,1,0:T(8,128)S(1)}, f32[2,64,1024]{2,1,0:T(8,128)}, u32[]{:S(2)}) copy-start(f32[2,64,1024]{2,1,0:T(8,128)} %param.6) | copy-start | bytes 1572868
  96.0 2.0 %copy-start.1 = (f32[512,512]{1,0:T(8,128)S(1)}, f32[512,512]{1,0:T(8,128)}, u32[]{:S(2)}) copy-start(f32[512,512]{1,0:T(8,128)} %param.9) | copy-start | bytes 3145732
  96.2 3.8 %copy-start.2 = (f32[512,512]{1,0:T(8,128)S(1)}, f32[512,512]{1,0:T(8,128)}, u32[]{:S(2)}) copy-start(f32[512,512]{1,0:T(8,128)} %param.11) | copy-start | bytes 3145732
Sparse Core Ops, SparseCore 0:
  9.6 73.3 all-gather.1
  104.5 37.3 reduce-scatter.1
